TPU v7x, 256 devices: a whole 4x4x8 slice. The times are simulated.
256 devices in a mesh: dp: 8 (over x, core), ulysses: 32 (over z, y).
Axes of the slice: x: 4, y: 4, z: 8, core: 2. Of those that a mesh axis runs over, the one named last changes fastest.
Arguments:
- normalized_input: bfloat16 [8, 4096, 4096], P('dp', 'ulysses'), may hold values from -6 to 6
- frozen_queries: bfloat16 [8, 4096, 4096], P('dp', 'ulysses'), may hold values from -40 to 40
- frozen_keys: bfloat16 [8, 4096, 4096], P('dp', 'ulysses'), may hold values from -8 to 8
- frozen_values: bfloat16 [8, 4096, 4096], P('dp', 'ulysses'), may hold values from -6 to 6
- output_gradient: bfloat16 [8, 4096, 4096], P('dp', 'ulysses'), may hold values from -0.125 to 0.125
- adapter_down_maps: bfloat16 [2, 4096, 64], replicated, may hold values from -0.09375 to 0.09375
- adapter_up_maps: bfloat16 [2, 64, 4096], replicated, may hold values from -0.75 to 0.75
- shifted: int32 [32], replicated, may hold values from 0 to 1, as said below
Outputs:
- grad_down: float32 [2, 4096, 64], P(None, 'ulysses')
- grad_up: float32 [2, 64, 4096], P(None, None, 'ulysses')
Inputs may be any that keep to these rules, and one draw needn't show every extreme that they name: `shifted`: exactly half of the 32 heads are marked 1, the others 0.
All inputs are finite; a program needn't handle non-finite values.
Results may differ from a plain program's by a relative error of at most 0.0067.
Values may be sent and summed in bfloat16 or wider, within the bound.
No kernel may reach another device: no remote copies, remote signals or barrier semaphores. Data moves between devices by JAX's collectives and lax.ppermute only.
A program may use at most 64 MiB of HBM per device.

v0:
```python
import math
import jax
import jax.numpy as jnp
from jax import lax
from jax.sharding import PartitionSpec as P

HEADS = 32
HD = 128
GROUP = 1024
SHIFT = 512
adapter_scale = 0.5


def group_backward(query_matrix, key_rows, value_matrix, upstream):
    factor = 1.0 / math.sqrt(query_matrix.shape[-1])
    scores = jnp.dot(query_matrix, key_rows.T, preferred_element_type=jnp.float32) * factor
    row_ids = lax.broadcasted_iota(jnp.int32, scores.shape, 0)
    column_ids = lax.broadcasted_iota(jnp.int32, scores.shape, 1)
    scores = jnp.where(column_ids <= row_ids, scores, -jnp.inf)
    row_top = jnp.max(scores, axis=1, keepdims=True)
    weights = jnp.exp(scores - row_top)
    row_total = jnp.sum(weights, axis=1, keepdims=True)
    attention = (weights / row_total).astype(jnp.bfloat16)
    output = jnp.dot(attention, value_matrix, preferred_element_type=jnp.float32)
    group_values = jnp.dot(attention.T, upstream, preferred_element_type=jnp.float32).astype(
        jnp.bfloat16
    )
    grad_attention = jnp.dot(upstream, value_matrix.T, preferred_element_type=jnp.float32)
    center = jnp.sum(upstream.astype(jnp.float32) * output, axis=1, keepdims=True)
    grad_scores = (attention.astype(jnp.float32) * (grad_attention - center)).astype(jnp.bfloat16)
    group_queries = (
        jnp.dot(grad_scores, key_rows, preferred_element_type=jnp.float32) * factor
    ).astype(jnp.bfloat16)
    return (group_queries, group_values)


def run_group(bundle):
    return group_backward(*bundle)


def head_backward(query_matrix, key_rows, value_matrix, upstream, flag):
    offset = flag * SHIFT
    head_width = query_matrix.shape[-1]
    blocks = tuple(
        (
            jnp.roll(member, -offset, axis=0).reshape(-1, GROUP, head_width)
            for member in (query_matrix, key_rows, value_matrix, upstream)
        )
    )
    grad_query, grad_value = lax.map(run_group, blocks)
    grad_query = jnp.roll(grad_query.reshape(-1, head_width), offset, axis=0)
    grad_value = jnp.roll(grad_value.reshape(-1, head_width), offset, axis=0)
    return (grad_query, grad_value)


def run_head(bundle):
    return head_backward(*bundle)


def per_device(
    normalized_input,
    frozen_queries,
    frozen_keys,
    frozen_values,
    output_gradient,
    adapter_down_maps,
    adapter_up_maps,
    shifted,
):
    seq_dev = normalized_input.shape[1]
    token_rows = normalized_input[0]
    rank_projection = jnp.einsum(
        "jp,kpi->kji", token_rows, adapter_down_maps, preferred_element_type=jnp.float32
    ).astype(jnp.bfloat16)
    raised_rows = jnp.einsum(
        "hgo,how->hgw", rank_projection, adapter_up_maps, preferred_element_type=jnp.float32
    )
    query_matrix = (frozen_queries[0].astype(jnp.float32) + adapter_scale * raised_rows[0]).astype(
        jnp.bfloat16
    )
    value_matrix = (frozen_values[0].astype(jnp.float32) + adapter_scale * raised_rows[1]).astype(
        jnp.bfloat16
    )
    rank_count = lax.axis_size("ulysses")
    local_heads = HEADS // rank_count
    local_width = local_heads * HD
    seq_total = seq_dev * rank_count

    def split_heads(member):
        return member.reshape(seq_dev, rank_count, local_width)

    arrived = (
        lax.all_to_all(
            split_heads(query_matrix), "ulysses", split_axis=1, concat_axis=0, tiled=True
        ),
        lax.all_to_all(
            split_heads(frozen_keys[0]), "ulysses", split_axis=1, concat_axis=0, tiled=True
        ),
        lax.all_to_all(
            split_heads(value_matrix), "ulysses", split_axis=1, concat_axis=0, tiled=True
        ),
        lax.all_to_all(
            split_heads(output_gradient[0]), "ulysses", split_axis=1, concat_axis=0, tiled=True
        ),
    )

    def per_head(member):
        return member.transpose(1, 0, 2)

    first_head = lax.axis_index("ulysses") * local_heads
    head_flags = lax.dynamic_slice_in_dim(shifted, first_head, local_heads)
    grad_query, grad_value = lax.map(
        run_head, tuple((per_head(member) for member in arrived)) + (head_flags,)
    )
    head_grads = (
        jnp.stack([grad_query, grad_value]).transpose(0, 2, 1, 3).reshape(2, seq_total, local_width)
    )
    returned = lax.all_to_all(
        head_grads.reshape(2, seq_total, 1, local_width),
        "ulysses",
        split_axis=1,
        concat_axis=2,
        tiled=True,
    )
    token_gradient = returned.reshape(2, seq_dev, rank_count * local_width)
    up_portion = adapter_scale * jnp.einsum(
        "vbw,vbe->vwe", rank_projection, token_gradient, preferred_element_type=jnp.float32
    )
    rank_backprop = jnp.einsum(
        "cne,cke->cnk", token_gradient, adapter_up_maps, preferred_element_type=jnp.float32
    ).astype(jnp.bfloat16)
    down_portion = adapter_scale * jnp.einsum(
        "yt,cyu->ctu", token_rows, rank_backprop, preferred_element_type=jnp.float32
    )
    down_share, up_share = (
        lax.psum_scatter(down_portion, "ulysses", scatter_dimension=1, tiled=True),
        lax.psum_scatter(up_portion, "ulysses", scatter_dimension=2, tiled=True),
    )
    grad_down, grad_up = lax.psum((down_share, up_share), "dp")
    return (grad_down, grad_up)


def solution(mesh):
    in_specs = (
        P("dp", "ulysses", None),
        P("dp", "ulysses", None),
        P("dp", "ulysses", None),
        P("dp", "ulysses", None),
        P("dp", "ulysses", None),
        P(),
        P(),
        P(),
    )
    out_specs = (P(None, "ulysses", None), P(None, None, "ulysses"))
    return jax.shard_map(
        per_device, mesh=mesh, in_specs=in_specs, out_specs=out_specs, check_vma=False
    )
```

profile of v0, /device:TPU:8, one launch (start us, length us, event | category | flops | bytes accessed | tf_op | source)
XLA Modules:
  0.0 790.9 jit_solution(1102728348083496166)
XLA Ops:
  13.2 11.7 %all-to-all-start = ((bf16[128,32,128]{2,0,1:T(8,128)(2,1)}), bf16[128,32,128]{2,0,1:T(8,128)(2,1)S(1)}, u32[]{:S(2)}, u32[]{:S(2)}) async-start(bf16[128,32,128]{2,0,1:T(8,128)(2,1)} %copy.23), calls=%async_computation | async-start | bytes 2097152 | tf_op jit(solution)/shard_map/all_to_all | solution.py:93
  26.5 26.4 %all-to-all-done = bf16[128,32,128]{2,0,1:T(8,128)(2,1)S(1)} async-done(((bf16[128,32,128]{2,0,1:T(8,128)(2,1)}), bf16[128,32,128]{2,0,1:T(8,128)(2,1)S(1)}, u32[]{:S(2)}, u32[]{:S(2)}) %all-to-all-start) | async-done | bytes 1048608 | tf_op jit(solution)/shard_map/all_to_all | solution.py:93
  52.9 5.6 all-to-all-start.3
  63.1 22.5 %all-to-all-done.3 = bf16[128,32,128]{2,0,1:T(8,128)(2,1)S(1)} async-done(((bf16[128,32,128]{2,0,1:T(8,128)(2,1)}), bf16[128,32,128]{2,0,1:T(8,128)(2,1)S(1)}, u32[]{:S(2)}, u32[]{:S(2)}) %all-to-all-start.3) | async-done | bytes 1048608 | tf_op jit(solution)/shard_map/all_to_all | solution.py:99
  85.5 5.6 all-to-all-start.1
  95.7 22.1 %all-to-all-done.1 = bf16[128,32,128]{2,0,1:T(8,128)(2,1)} async-done(((bf16[128,32,128]{2,0,1:T(8,128)(2,1)}), bf16[128,32,128]{2,0,1:T(8,128)(2,1)}, u32[]{:S(2)}, u32[]{:S(2)}) %all-to-all-start.1) | async-done | bytes 1048608 | tf_op jit(solution)/shard_map/all_to_all | solution.py:96
  117.7 5.6 all-to-all-start.2
  124.9 4.6 fusion.42
  129.5 4.6 fusion.39
  134.2 2.9 fusion.41
  137.1 12.6 %all-to-all-done.2 = bf16[128,32,128]{2,0,1:T(8,128)(2,1)} async-done(((bf16[128,32,128]{2,0,1:T(8,128)(2,1)}), bf16[128,32,128]{2,0,1:T(8,128)(2,1)}, u32[]{:S(2)}, u32[]{:S(2)}) %all-to-all-start.2) | async-done | bytes 1048608 | tf_op jit(solution)/shard_map/all_to_all | solution.py:102
  149.7 2.9 fusion.40
  152.6 49.9 %while.21 = (s32[]{:T(128)}, bf16[4,1024,128]{2,1,0:T(8,128)(2,1)}, bf16[4,1024,128]{2,1,0:T(8,128)(2,1)}, bf16[4,1024,128]{2,1,0:T(8,128)(2,1)}, bf16[4,1024,12...) while((s32[]{:T(128)}, bf16[4,1024,128]{2,1,0:T(8,128)(2,1)}, ...), condition=%wide.region_4.6_spmd, body=%wide.region_0.5_spmd.sunk | while | flops 1362883584 | bytes 24674904 | solution.py:50
  158.8 3.9 fusion.79
  171.3 3.9 fusion.79
  183.8 3.9 fusion.79
  196.2 3.9 fusion.79
  205.3 17.8 %copy.30 = bf16[2,4096,1,128]{3,0,2,1:T(2,128)(2,1)S(1)} copy(bf16[2,4096,1,128]{3,1,0,2:T(8,128)(2,1)S(1)} %maximum_bitcast_fusion) | data formatting | bytes 4194304 | tf_op jit(solution)/shard_map/transpose | solution.py:116
  223.1 53.6 %all_to_all.75 = bf16[2,4096,1,128]{3,0,2,1:T(2,128)(2,1)S(1)} all-to-all(bf16[2,4096,1,128]{3,0,2,1:T(2,128)(2,1)S(1)} %copy.30), channel_id=1, replica_groups=mesh['dp'=8,'ulysses'=32] {'ulysses'}, dimensions={1} | all-to-all | bytes 4194304 | tf_op jit(solution)/shard_map/all_to_all | solution.py:118
  279.7 2.8 reshape.69
  284.4 3.8 fusion.30
  288.2 208.4 %reduce-scatter.5.cloned.1.call-done = f32[2,64,128]{2,1,0:T(8,128)} async-done(((f32[2,64,4096]{2,1,0:T(8,128)}), f32[2,64,128]{2,1,0:T(8,128)}) %reduce-scatter.5.cloned.1.call-update) | async-done | bytes 65552 | tf_op jit(solution)/shard_map/reduce_scatter | solution.py:137
  496.6 218.7 %reduce-scatter.3.cloned.1.call-done = f32[2,128,64]{1,2,0:T(8,128)} async-done(((f32[2,4096,64]{1,2,0:T(8,128)}), f32[2,128,64]{1,2,0:T(8,128)}) %reduce-scatter.3.cloned.1.call-update) | async-done | bytes 65552 | tf_op jit(solution)/shard_map/reduce_scatter | solution.py:136
  715.4 66.0 %all-reduce.3.cloned.1.call-done = (f32[2,128,64]{1,2,0:T(8,128)}, f32[2,64,128]{2,1,0:T(8,128)}) async-done(((f32[2,128,64]{1,2,0:T(8,128)}, f32[2,64,128]{2,1,0:T(8,128)}), (f32[2,128,64]{1,2,0:T(8,128)}, f32[2,64,128]{2,1,0:T(8,128)})) %all-reduce.3.cloned.1.call-update) | async-done | bytes 131088 | tf_op jit(solution)/shard_map/psum | solution.py:139
  (63 shorter events, 62.3 us)
Async XLA Ops:
  7.2 2.1 copy-start
  9.3 1.2 copy-start.1
  9.3 1.5 copy-start.2
  13.2 39.8 %all-to-all-start = ((bf16[128,32,128]{2,0,1:T(8,128)(2,1)}), bf16[128,32,128]{2,0,1:T(8,128)(2,1)S(1)}, u32[]{:S(2)}, u32[]{:S(2)}) async-start(bf16[128,32,128]{2,0,1:T(8,128)(2,1)} %copy.23), calls=%async_computation | async-start | bytes 2097152 | tf_op jit(solution)/shard_map/all_to_all | solution.py:93
  52.9 32.6 %all-to-all-start.3 = ((bf16[128,32,128]{2,0,1:T(8,128)(2,1)}), bf16[128,32,128]{2,0,1:T(8,128)(2,1)S(1)}, u32[]{:S(2)}, u32[]{:S(2)}) async-start(bf16[128,32,128]{2,0,1:T(8,128)(2,1)} %copy.28), calls=%async_computation.3 | async-start | bytes 2097152 | tf_op jit(solution)/shard_map/all_to_all | solution.py:99
  85.5 32.2 %all-to-all-start.1 = ((bf16[128,32,128]{2,0,1:T(8,128)(2,1)}), bf16[128,32,128]{2,0,1:T(8,128)(2,1)}, u32[]{:S(2)}, u32[]{:S(2)}) async-start(bf16[128,32,128]{2,0,1:T(8,128)(2,1)} %copy.25), calls=%async_computation.1 | async-start | bytes 2097152 | tf_op jit(solution)/shard_map/all_to_all | solution.py:96
  93.4 30.2 %copy-start.3 = (s32[32]{0:T(128)S(1)}, s32[32]{0:T(128)}, u32[]{:S(2)}) copy-start(s32[32]{0:T(128)} %param.19) | copy-start | bytes 388
  117.7 31.9 %all-to-all-start.2 = ((bf16[128,32,128]{2,0,1:T(8,128)(2,1)}), bf16[128,32,128]{2,0,1:T(8,128)(2,1)}, u32[]{:S(2)}, u32[]{:S(2)}) async-start(bf16[128,32,128]{2,0,1:T(8,128)(2,1)} %copy.27), calls=%async_computation.2 | async-start | bytes 2097152 | tf_op jit(solution)/shard_map/all_to_all | solution.py:102
  123.4 373.2 %reduce-scatter.5.cloned.1.call-start = ((), (), s32[]{:S(2)}) async-start(), calls=%async_computation.8 | async-start | bytes 2162688 | tf_op jit(solution)/shard_map/reduce_scatter | solution.py:137
  284.3 431.0 %reduce-scatter.3.cloned.1.call-start = ((), (), s32[]{:S(2)}) async-start(), calls=%async_computation.7 | async-start | bytes 2162688 | tf_op jit(solution)/shard_map/reduce_scatter | solution.py:136
  288.2 493.2 %all-reduce.3.cloned.1.call-start = ((), (), s32[]{:S(2)}) async-start(), calls=%async_computation.9 | async-start | bytes 262144 | tf_op jit(solution)/shard_map/psum | solution.py:139
Sparse Core Ops, SparseCore 0:
  284.4 212.1 reduce-scatter.4
  500.9 214.3 reduce-scatter.2
  717.7 63.6 all-reduce.2
where the time goes:
time: 792 us; the launch traced here: 791 us
  waiting for transfers between devices  577 us (73%)
  blocking collectives  53.6 us (7%)
  local copies, waits for them, and re-layouts  47.6 us (6%)
  matrix products  46.5 us (6%)
  starting transfers between devices  28.8 us (4%)
  other arithmetic  23 us (3%)
  between operations  14.6 us (2%)
    reduce_scatter x1, waiting for transfers between devices, per_device(): lax.psum_scatter(down_portion, 'ulysses', scatter_dimension=1, tiled=True)  219 us
    reduce_scatter x1, waiting for transfers between devices, per_device(): lax.psum_scatter(up_portion, 'ulysses', scatter_dimension=2, tiled=True)  208 us
    psum x1, waiting for transfers between devices, per_device(): grad_down, grad_up = lax.psum((down_share, up_share), 'dp')  66 us
    all_to_all x1, blocking collectives, per_device(): lax.all_to_all(head_grads.reshape(2, seq_total, 1, local_width), 'ulysses...  53.6 us
    all_to_all x1, waiting for transfers between devices, per_device(): lax.all_to_all(split_heads(query_matrix), 'ulysses', split_axis=1, concat...  26.4 us
    all_to_all x1, waiting for transfers between devices, per_device(): lax.all_to_all(split_heads(value_matrix), 'ulysses', split_axis=1, concat...  22.5 us
    all_to_all x1, waiting for transfers between devices, per_device(): lax.all_to_all(split_heads(frozen_keys[0]), 'ulysses', split_axis=1, conc...  22.1 us
    transpose x1, local copies, waits for them, and re-layouts, per_device(): jnp.stack([grad_query, grad_value]).transpose(0, 2, 1, 3)  17.8 us
  transfers between devices with their start and end apart: 7, of which 7 were waited for; matrix products, arithmetic and copies ran while one was open for 3% of the time, Pallas kernels for 0%

commit v1 on v0

--- a/solution.py
+++ b/solution.py
@@ -90,8 +90,14 @@
         return member.reshape(seq_dev, rank_count, local_width)
 
     arrived = (
-        lax.all_to_all(
-            split_heads(query_matrix), "ulysses", split_axis=1, concat_axis=0, tiled=True
+        jnp.concatenate(
+            lax.all_to_all(
+                jnp.stack(jnp.split(split_heads(query_matrix), lax.axis_size("ulysses"), axis=1)),
+                "ulysses",
+                0,
+                0,
+            ),
+            axis=0,
         ),
         lax.all_to_all(
             split_heads(frozen_keys[0]), "ulysses", split_axis=1, concat_axis=0, tiled=True

time: 792 us -> 812 us (1.025)
  local copies, waits for them, and re-layouts: 47.6 us -> 67.6 us
    unnamed x14 -> x45, local copies, waits for them, and re-layouts: 8.75 us -> 27.6 us
where the time goes in v1:
time: 812 us; the launch traced here: 811 us
  waiting for transfers between devices  577 us (71%)
  local copies, waits for them, and re-layouts  67.6 us (8%)
  blocking collectives  53.6 us (7%)
  matrix products  46.5 us (6%)
  starting transfers between devices  28.8 us (4%)
  other arithmetic  23 us (3%)
  between operations  14.6 us (2%)
    reduce_scatter x1, waiting for transfers between devices, per_device(): lax.psum_scatter(down_portion, 'ulysses', scatter_dimension=1, tiled=True)  219 us
    reduce_scatter x1, waiting for transfers between devices, per_device(): lax.psum_scatter(up_portion, 'ulysses', scatter_dimension=2, tiled=True)  208 us
    psum x1, waiting for transfers between devices, per_device(): grad_down, grad_up = lax.psum((down_share, up_share), 'dp')  66 us
    all_to_all x1, blocking collectives, per_device(): lax.all_to_all(head_grads.reshape(2, seq_total, 1, local_width), 'ulysses...  53.6 us
    unnamed x45, local copies, waits for them, and re-layouts  27.6 us
    all_to_all x1, waiting for transfers between devices, per_device(): lax.all_to_all(jnp.stack(jnp.split(split_heads(query_matrix), lax.axis_si...  26.4 us
    all_to_all x1, waiting for transfers between devices, per_device(): lax.all_to_all(split_heads(value_matrix), 'ulysses', split_axis=1, concat...  22.5 us
    all_to_all x1, waiting for transfers between devices, per_device(): lax.all_to_all(split_heads(frozen_keys[0]), 'ulysses', split_axis=1, conc...  22.1 us
  transfers between devices with their start and end apart: 7, of which 7 were waited for; matrix products, arithmetic and copies ran while one was open for 3% of the time, Pallas kernels for 0%

profile of v1, /device:TPU:8, one launch (start us, length us, event | category | flops | bytes accessed | tf_op | source)
XLA Modules:
  0.0 810.8 jit_solution(10521754123838620198)
XLA Ops:
  33.3 11.7 %all-to-all-start = ((bf16[32,128,1,128]{3,1,2,0:T(8,128)(2,1)}), bf16[32,128,1,128]{3,1,2,0:T(8,128)(2,1)S(1)}, u32[]{:S(2)}, u32[]{:S(2)}) async-start(bf16[32,128,1,128]{3,1,2,0:T(8,128)(2,1)} %constant_dynamic-update-slice_fusion), calls=%async_computation | async-start | bytes 2097152 | tf_op jit(solution)/shard_map/all_to_all | solution.py:94
  46.7 26.4 %all-to-all-done = bf16[32,128,1,128]{3,1,2,0:T(8,128)(2,1)S(1)} async-done(((bf16[32,128,1,128]{3,1,2,0:T(8,128)(2,1)}), bf16[32,128,1,128]{3,1,2,0:T(8,128)(2,1)S(1)}, u32[]{:S(2)}, u32[]{:S(2)}) %all-to-all-start) | async-done | bytes 1048608 | tf_op jit(solution)/shard_map/all_to_all | solution.py:94
  73.1 5.6 all-to-all-start.3
  83.2 22.5 %all-to-all-done.3 = bf16[128,32,128]{2,0,1:T(8,128)(2,1)S(1)} async-done(((bf16[128,32,128]{2,0,1:T(8,128)(2,1)}), bf16[128,32,128]{2,0,1:T(8,128)(2,1)S(1)}, u32[]{:S(2)}, u32[]{:S(2)}) %all-to-all-start.3) | async-done | bytes 1048608 | tf_op jit(solution)/shard_map/all_to_all | solution.py:105
  105.7 5.6 all-to-all-start.1
  115.8 22.1 %all-to-all-done.1 = bf16[128,32,128]{2,0,1:T(8,128)(2,1)} async-done(((bf16[128,32,128]{2,0,1:T(8,128)(2,1)}), bf16[128,32,128]{2,0,1:T(8,128)(2,1)}, u32[]{:S(2)}, u32[]{:S(2)}) %all-to-all-start.1) | async-done | bytes 1048608 | tf_op jit(solution)/shard_map/all_to_all | solution.py:102
  137.9 5.6 all-to-all-start.2
  145.1 4.6 fusion.42
  149.7 4.6 fusion.39
  154.3 2.9 fusion.41
  157.2 12.6 %all-to-all-done.2 = bf16[128,32,128]{2,0,1:T(8,128)(2,1)} async-done(((bf16[128,32,128]{2,0,1:T(8,128)(2,1)}), bf16[128,32,128]{2,0,1:T(8,128)(2,1)}, u32[]{:S(2)}, u32[]{:S(2)}) %all-to-all-start.2) | async-done | bytes 1048608 | tf_op jit(solution)/shard_map/all_to_all | solution.py:108
  169.8 2.9 fusion.40
  172.7 49.9 %while.21 = (s32[]{:T(128)}, bf16[4,1024,128]{2,1,0:T(8,128)(2,1)}, bf16[4,1024,128]{2,1,0:T(8,128)(2,1)}, bf16[4,1024,128]{2,1,0:T(8,128)(2,1)}, bf16[4,1024,12...) while((s32[]{:T(128)}, bf16[4,1024,128]{2,1,0:T(8,128)(2,1)}, ...), condition=%wide.region_4.6_spmd, body=%wide.region_0.5_spmd.sunk | while | flops 1362883584 | bytes 24674904 | solution.py:50
  178.9 3.9 fusion.81
  191.4 3.9 fusion.81
  203.9 3.9 fusion.81
  216.4 3.9 fusion.81
  225.4 17.8 %copy.154 = bf16[2,4096,1,128]{3,0,2,1:T(2,128)(2,1)S(1)} copy(bf16[2,4096,1,128]{3,1,0,2:T(8,128)(2,1)S(1)} %maximum_bitcast_fusion) | data formatting | bytes 4194304 | tf_op jit(solution)/shard_map/transpose | solution.py:122
  243.3 53.6 %all_to_all.65 = bf16[2,4096,1,128]{3,0,2,1:T(2,128)(2,1)S(1)} all-to-all(bf16[2,4096,1,128]{3,0,2,1:T(2,128)(2,1)S(1)} %copy.154), channel_id=1, replica_groups=mesh['dp'=8,'ulysses'=32] {'ulysses'}, dimensions={1} | all-to-all | bytes 4194304 | tf_op jit(solution)/shard_map/all_to_all | solution.py:124
  299.8 2.8 reshape.68
  304.5 3.8 fusion.30
  308.3 208.3 %reduce-scatter.5.cloned.1.call-done = f32[2,64,128]{2,1,0:T(8,128)} async-done(((f32[2,64,4096]{2,1,0:T(8,128)}), f32[2,64,128]{2,1,0:T(8,128)}) %reduce-scatter.5.cloned.1.call-update) | async-done | bytes 65552 | tf_op jit(solution)/shard_map/reduce_scatter | solution.py:143
  516.7 218.7 %reduce-scatter.3.cloned.1.call-done = f32[2,128,64]{1,2,0:T(8,128)} async-done(((f32[2,4096,64]{1,2,0:T(8,128)}), f32[2,128,64]{1,2,0:T(8,128)}) %reduce-scatter.3.cloned.1.call-update) | async-done | bytes 65552 | tf_op jit(solution)/shard_map/reduce_scatter | solution.py:142
  735.4 66.0 %all-reduce.3.cloned.1.call-done = (f32[2,128,64]{1,2,0:T(8,128)}, f32[2,64,128]{2,1,0:T(8,128)}) async-done(((f32[2,128,64]{1,2,0:T(8,128)}, f32[2,64,128]{2,1,0:T(8,128)}), (f32[2,128,64]{1,2,0:T(8,128)}, f32[2,64,128]{2,1,0:T(8,128)})) %all-reduce.3.cloned.1.call-update) | async-done | bytes 131088 | tf_op jit(solution)/shard_map/psum | solution.py:145
  (96 shorter events, 82.4 us)
Async XLA Ops:
  7.2 2.1 copy-start
  9.3 1.2 copy-start.1
  9.3 1.5 copy-start.2
  33.3 39.8 %all-to-all-start = ((bf16[32,128,1,128]{3,1,2,0:T(8,128)(2,1)}), bf16[32,128,1,128]{3,1,2,0:T(8,128)(2,1)S(1)}, u32[]{:S(2)}, u32[]{:S(2)}) async-start(bf16[32,128,1,128]{3,1,2,0:T(8,128)(2,1)} %constant_dynamic-update-slice_fusion), calls=%async_computation | async-start | bytes 2097152 | tf_op jit(solution)/shard_map/all_to_all | solution.py:94
  73.1 32.6 %all-to-all-start.3 = ((bf16[128,32,128]{2,0,1:T(8,128)(2,1)}), bf16[128,32,128]{2,0,1:T(8,128)(2,1)S(1)}, u32[]{:S(2)}, u32[]{:S(2)}) async-start(bf16[128,32,128]{2,0,1:T(8,128)(2,1)} %copy.152), calls=%async_computation.3 | async-start | bytes 2097152 | tf_op jit(solution)/shard_map/all_to_all | solution.py:105
  105.7 32.2 %all-to-all-start.1 = ((bf16[128,32,128]{2,0,1:T(8,128)(2,1)}), bf16[128,32,128]{2,0,1:T(8,128)(2,1)}, u32[]{:S(2)}, u32[]{:S(2)}) async-start(bf16[128,32,128]{2,0,1:T(8,128)(2,1)} %copy.149), calls=%async_computation.1 | async-start | bytes 2097152 | tf_op jit(solution)/shard_map/all_to_all | solution.py:102
  113.5 30.2 %copy-start.3 = (s32[32]{0:T(128)S(1)}, s32[32]{0:T(128)}, u32[]{:S(2)}) copy-start(s32[32]{0:T(128)} %param.19) | copy-start | bytes 388
  137.9 31.9 %all-to-all-start.2 = ((bf16[128,32,128]{2,0,1:T(8,128)(2,1)}), bf16[128,32,128]{2,0,1:T(8,128)(2,1)}, u32[]{:S(2)}, u32[]{:S(2)}) async-start(bf16[128,32,128]{2,0,1:T(8,128)(2,1)} %copy.151), calls=%async_computation.2 | async-start | bytes 2097152 | tf_op jit(solution)/shard_map/all_to_all | solution.py:108
  143.5 373.2 %reduce-scatter.5.cloned.1.call-start = ((), (), s32[]{:S(2)}) async-start(), calls=%async_computation.8 | async-start | bytes 2162688 | tf_op jit(solution)/shard_map/reduce_scatter | solution.py:143
  304.4 430.9 %reduce-scatter.3.cloned.1.call-start = ((), (), s32[]{:S(2)}) async-start(), calls=%async_computation.7 | async-start | bytes 2162688 | tf_op jit(solution)/shard_map/reduce_scatter | solution.py:142
  308.3 493.1 %all-reduce.3.cloned.1.call-start = ((), (), s32[]{:S(2)}) async-start(), calls=%async_computation.9 | async-start | bytes 262144 | tf_op jit(solution)/shard_map/psum | solution.py:145
Sparse Core Ops, SparseCore 0:
  304.5 212.0 reduce-scatter.4
  521.0 214.3 reduce-scatter.2
  737.7 63.5 all-reduce.2
